TPU v7x, 32 devices: a whole 2x2x4 slice. The times are simulated.
32 devices in a mesh: dp: 4 (over z), lib: 8 (over y, x, core).
Axes of the slice: x: 2, y: 2, z: 4, core: 2. Of those that a mesh axis runs over, the one named last changes fastest.
Arguments:
- spectra: bfloat16 [12288, 512], P(('dp', 'lib')), may hold values from -6 to 6
- w_proj: bfloat16 [512, 512], replicated, may hold values from -0.25 to 0.25
- fixed_library_matrix: bfloat16 [8192, 512], P('lib')
- mol_rows: bfloat16 [65536, 512], P(('dp', 'lib'))
- cand_ids: int32 [12288, 4], P(('dp', 'lib')), may hold values from 0 to 65535, as said below
- iso_count: int32 [12288], P(('dp', 'lib')), may hold values from 1 to 3
Outputs:
- grad_w: float32 [512, 512], replicated
- grad_mol: float32 [65536, 512], P(('dp', 'lib'))
- loss: float32 [], replicated
Inputs may be any that keep to these rules, and one draw needn't show every extreme that they name: cand_ids of a spectrum on device dp, lib (in dp+lib order) name rows of the dp group's molecules: id // 2048 // 8 equals dp. Over one device's 1536 slots (all columns, live or not), at most 384 name rows whose (id // 2048) % 8 is one lib index, and exactly 384 for some lib index on every device.
All inputs are finite; a program needn't handle non-finite values.
Results may differ from a plain program's by a relative error of at most 0.0074.
Values may be sent and summed in bfloat16 or wider, within the bound.
No kernel may reach another device: no remote copies, remote signals or barrier semaphores. Data moves between devices by JAX's collectives and lax.ppermute only.
A program may use at most 64 MiB of HBM per device.

v0:
```python
import jax
import jax.numpy as jnp
from jax import lax
from jax.sharding import PartitionSpec as P

sharpness_divisor = 0.07


def absorb(state, block, spectrum_encoding):
    running_max, running_sum, derivative_tally = state
    scores = (
        lax.dot_general(
            spectrum_encoding, block, (((1,), (1,)), ((), ())), preferred_element_type=jnp.float32
        )
        / sharpness_divisor
    )
    new_max = jnp.maximum(running_max, jnp.max(scores, axis=1))
    inverse_sharpness = jnp.exp(running_max - new_max)
    weights = jnp.exp(scores - new_max[:, None])
    running_sum = running_sum * inverse_sharpness + jnp.sum(weights, axis=1)
    derivative_tally = derivative_tally * inverse_sharpness[:, None] + jnp.dot(
        weights.astype(jnp.bfloat16), block, preferred_element_type=jnp.float32
    )
    return (new_max, running_sum, derivative_tally)


def per_device(spectra, w_proj, fixed_library_matrix, mol_rows, cand_ids, iso_count):
    q_rows = spectra.shape[0]
    width = spectra.shape[1]
    mol_count = mol_rows.shape[0]
    bank_count = fixed_library_matrix.shape[0]
    lib_size = lax.axis_size("lib")
    columns = cand_ids.shape[1]
    slot_count = q_rows * columns
    capacity = 2 * slot_count // lib_size
    u_proj = jnp.dot(spectra, w_proj, preferred_element_type=jnp.float32)
    norm = jnp.sqrt(jnp.sum(u_proj * u_proj, axis=1, keepdims=True) + 1e-06)
    normalized_spectrum_matrix = u_proj / norm
    spectrum_encoding = normalized_spectrum_matrix.astype(jnp.bfloat16)
    flat_ids = cand_ids.reshape(-1)
    owner = flat_ids // mol_count % lib_size
    local_row = flat_ids % mol_count
    onehot = (owner[:, None] == jnp.arange(lib_size, dtype=jnp.int32)[None, :]).astype(jnp.int32)
    before = jnp.cumsum(onehot, axis=0) - onehot
    position = owner * capacity + jnp.sum(before * onehot, axis=1)
    requests = jnp.zeros((lib_size * capacity,), jnp.int32).at[position].set(local_row)
    requests = requests.reshape(lib_size, capacity)
    received = lax.all_to_all(requests, "lib", split_axis=0, concat_axis=0, tiled=True)
    fetched = mol_rows[received]
    returned = lax.all_to_all(fetched, "lib", split_axis=0, concat_axis=0, tiled=True)
    contender_embedding_matrix = returned.reshape(lib_size * capacity, width)[position].reshape(
        q_rows, columns, width
    )
    candidate_float_rows = contender_embedding_matrix.astype(jnp.float32)
    column = jnp.arange(columns, dtype=jnp.int32)[None, :]
    live = column <= iso_count[:, None]
    contender_similarity_values = (
        jnp.einsum(
            "ti,tmi->tm",
            spectrum_encoding,
            contender_embedding_matrix,
            preferred_element_type=jnp.float32,
        )
        / sharpness_divisor
    )
    cand_max = jnp.max(jnp.where(live, contender_similarity_values, -1e30), axis=1)
    cand_weights = jnp.where(live, jnp.exp(contender_similarity_values - cand_max[:, None]), 0.0)
    start_state = (
        cand_max,
        jnp.sum(cand_weights, axis=1),
        jnp.einsum("qk,qkd->qd", cand_weights, candidate_float_rows),
    )
    piece = lax.all_gather(fixed_library_matrix, "lib", axis=0, tiled=True)
    stacked = piece.reshape(piece.shape[0] // bank_count, bank_count, width)

    def inner(current, block):
        return (absorb(current, block, spectrum_encoding), 0)

    result, unused = lax.scan(inner, start_state, stacked)
    top, objective_aggregate, derivative_tally = result
    lse = top + jnp.log(objective_aggregate)
    scaled_cand = jnp.where(live, jnp.exp(contender_similarity_values - top[:, None]), 0.0)
    loss_terms = jnp.sum(lse - contender_similarity_values[:, 0])
    spectrum_derivative = (
        derivative_tally / objective_aggregate[:, None] - candidate_float_rows[:, 0, :]
    ) / sharpness_divisor
    grad_u = (
        (
            spectrum_derivative
            - normalized_spectrum_matrix
            * jnp.sum(normalized_spectrum_matrix * spectrum_derivative, axis=1, keepdims=True)
        )
        / norm
    ).astype(jnp.bfloat16)
    grad_local = jnp.dot(spectra.T, grad_u, preferred_element_type=jnp.float32)
    first = (column == 0).astype(jnp.float32)
    inverse_sharpness = jnp.where(live, scaled_cand / objective_aggregate[:, None] - first, 0.0)
    contender_derivative = (
        inverse_sharpness[:, :, None] * normalized_spectrum_matrix[:, None, :] / sharpness_divisor
    ).astype(jnp.bfloat16)
    outgoing = (
        jnp.zeros((lib_size * capacity, width), jnp.bfloat16)
        .at[position]
        .set(contender_derivative.reshape(slot_count, width))
    )
    incoming = lax.all_to_all(
        outgoing.reshape(lib_size, capacity, width), "lib", split_axis=0, concat_axis=0, tiled=True
    )
    grad_mol = (
        jnp.zeros((mol_count, width), jnp.float32)
        .at[received.reshape(-1)]
        .add(incoming.reshape(-1, width).astype(jnp.float32))
    )
    grad_w, loss_sum = lax.psum((grad_local, loss_terms), ("dp", "lib"))
    loss = loss_sum / (q_rows * lax.axis_size("dp") * lib_size)
    return (grad_w, grad_mol, loss)


def solution(mesh):
    placed = (
        P(("dp", "lib"), None),
        P(),
        P("lib", None),
        P(("dp", "lib"), None),
        P(("dp", "lib"), None),
        P(("dp", "lib")),
    )
    return jax.shard_map(
        per_device,
        mesh=mesh,
        in_specs=placed,
        out_specs=(P(), P(("dp", "lib"), None), P()),
        check_vma=False,
    )
```

profile of v0, /device:TPU:0, one launch (start us, length us, event | category | flops | bytes accessed | tf_op | source)
XLA Modules:
  0.0 341.9 jit_solution(17671516270576667808)
XLA Ops:
  7.2 0.7 all-gather.2.cloned.1.call-update
  7.9 0.8 copy.10
  9.2 2.3 reduce-window.6
  12.2 6.2 %scatter_custom_fusion = s32[3072]{0:T(1024)S(1)} fusion(s32[1536]{0:T(1024)S(1)} %fusion.31, s32[1536]{0:T(1024)S(1)} %get-tuple-element.64, s32[]{:T(128)} %copy.49), kind=kCustom, calls=%fused_computation.91 | custom fusion | bytes 12292 | tf_op jit(solution)/shard_map/scatter | solution.py:46
  18.4 10.0 %all_to_all.22 = s32[8,1,384]{2,1,0:T(1,128)S(1)} all-to-all(s32[8,1,384]{2,1,0:T(1,128)S(1)} %bitcast.85), channel_id=1, replica_groups=mesh['dp'=4,'lib'=8] {'lib'}, dimensions={0} | all-to-all | bytes 24576 | tf_op jit(solution)/shard_map/all_to_all | solution.py:48
  28.4 13.3 %gather_fusion = bf16[3072,512]{1,0:T(8,128)(2,1)} fusion(bf16[2048,512]{1,0:T(8,128)(2,1)S(1)} %copy-done, s32[3072]{0:T(1024)S(1)} %broadcast_clamp_fusion), kind=kCustom, calls=%fused_computation | custom fusion | bytes 6303744 | tf_op jit(solution)/shard_map/gather | solution.py:49
  41.7 4.8 %all-to-all-start.1 = ((bf16[8,384,512]{2,1,0:T(8,128)(2,1)}), bf16[8,384,512]{2,1,0:T(8,128)(2,1)}, u32[]{:S(2)}, u32[]{:S(2)}) async-start(bf16[8,384,512]{2,1,0:T(8,128)(2,1)} %bitcast.83), calls=%async_computation.1 | async-start | bytes 6291456 | tf_op jit(solution)/shard_map/all_to_all | solution.py:50
  46.5 0.5 multiply_reduce_fusion.1
  47.1 0.9 copy-done.1
  48.0 2.2 mul.68
  50.2 4.9 %mul.69 = f32[1536,512]{1,0:T(8,128)} reshape(f32[384,4,512]{2,1,0:T(4,128)} %mul.68) | data formatting | bytes 6291456 | tf_op jit(solution)/shard_map/mul | solution.py:99
  55.1 44.7 %all-to-all-done.1 = bf16[8,384,512]{2,1,0:T(8,128)(2,1)} async-done(((bf16[8,384,512]{2,1,0:T(8,128)(2,1)}), bf16[8,384,512]{2,1,0:T(8,128)(2,1)}, u32[]{:S(2)}, u32[]{:S(2)}) %all-to-all-start.1) | async-done | bytes 3145760 | tf_op jit(solution)/shard_map/all_to_all | solution.py:50
  99.8 7.8 %gather_fusion.1 = bf16[1536,512]{1,0:T(8,128)(2,1)} fusion(bf16[3072,512]{1,0:T(8,128)(2,1)} %bitcast.7, s32[2048]{0:T(1024)S(1)} %pad_clamp_fusion), kind=kCustom, calls=%fused_computation.1 | custom fusion | bytes 3151872 | tf_op jit(solution)/shard_map/gather | solution.py:51
  107.6 3.5 %reshape.274 = bf16[384,4,512]{2,1,0:T(4,128)(2,1)} reshape(bf16[1536,512]{1,0:T(8,128)(2,1)} %gather_fusion.1) | data formatting | bytes 3145728 | tf_op jit(solution)/shard_map/reshape | solution.py:51
  111.1 2.8 fusion.18
  114.3 2.4 fusion.43
  116.8 34.0 %while.14 = (s32[]{:T(128)}, f32[384]{0:T(512)S(1)}, f32[384]{0:T(512)S(1)}, f32[384,512]{1,0:T(8,128)S(1)}, bf16[8,1024,512]{2,1,0:T(8,128)(2,1)}, /*index=5*/bf16[384,512]{1,0:T(8,128)(2,1)S(1)}, s32[]{:T(128)}) while((s32[]{:T(128)}, f32[384]{0:T(512)S(1)}, f32[384]{0:T(512)S(1)}, f32[384,512]{1,0:T(8,128)S(1)}, ...), condition=%wide.region_10.11_spmd, body=%wide.region_7.10_spmd.sunk | while | flops 808059648 | bytes 8806493 | solution.py:79
  116.8 2.0 fusion.59
  118.8 0.3 fusion.60
  119.1 1.9 convolution_add_fusion.2
  121.1 2.0 fusion.59
  123.0 0.3 fusion.60
  123.3 1.9 convolution_add_fusion.2
  125.3 2.0 fusion.59
  127.3 0.3 fusion.60
  127.6 1.9 convolution_add_fusion.2
  129.6 2.0 fusion.59
  131.8 1.9 convolution_add_fusion.2
  133.8 2.0 fusion.59
  136.1 1.9 convolution_add_fusion.2
  138.1 2.0 fusion.59
  140.0 0.3 fusion.60
  140.4 1.9 convolution_add_fusion.2
  142.3 2.0 fusion.59
  144.6 1.9 convolution_add_fusion.2
  146.6 2.0 fusion.59
  148.5 0.3 fusion.60
  148.9 1.9 convolution_add_fusion.2
  151.2 10.7 %scatter_custom_fusion.1 = bf16[3072,512]{1,0:T(8,128)(2,1)} fusion(s32[1536]{0:T(1024)S(1)} %fusion.31, f32[1536,512]{1,0:T(8,128)} %mul.69, f32[]{:T(128)} %constant.84.clone.1, f32[1536]{0:T(1024)S(1)} %mul.66, bf16[]{:T(256)} %constant.87.clone.1), kind=kCustom, calls=%fused_computation.23 | custom fusion | flops 2359296 | bytes 6299654 | tf_op jit(solution)/shard_map/scatter | solution.py:104
  161.9 4.4 %all-to-all-start.2 = ((bf16[8,384,512]{2,1,0:T(8,128)(2,1)}), bf16[8,384,512]{2,1,0:T(8,128)(2,1)}, u32[]{:S(2)}, u32[]{:S(2)}) async-start(bf16[8,384,512]{2,1,0:T(8,128)(2,1)} %bitcast.82), calls=%async_computation.2 | async-start | bytes 6291456 | tf_op jit(solution)/shard_map/all_to_all | solution.py:106
  166.6 2.0 slice.22
  168.7 1.4 multiply_reduce_fusion
  170.1 1.7 convolution_bitcast_fusion
  171.8 0.6 subtract_reduce_fusion
  172.5 67.0 %psum.15 = f32[]{:T(128)} all-reduce(f32[]{:T(128)} %subtract_reduce_fusion), channel_id=1, replica_groups=mesh['dp'=4,'lib'=8] {'dp','lib'}, use_global_device_ids=true, to_apply=%region_16.17 | all-reduce | flops 1 | bytes 8 | tf_op jit(solution)/shard_map/psum | solution.py:114
  240.2 68.1 %all-reduce.2.cloned.1.call-done = f32[512,512]{0,1:T(8,128)} async-done(((f32[512,512]{0,1:T(8,128)}), f32[512,512]{0,1:T(8,128)}) %all-reduce.2.cloned.1.call-update) | async-done | bytes 1048592 | tf_op jit(solution)/shard_map/psum | solution.py:114
  308.2 2.5 copy.15
  310.7 23.2 %scatter_custom_fusion.2 = f32[2048,512]{1,0:T(8,128)} fusion(s32[3072]{0:T(1024)S(1)} %bitcast.88, bf16[3072,512]{1,0:T(8,128)(2,1)} %bitcast.19, f32[]{:T(128)} %constant.73.clone.1), kind=kCustom, calls=%fused_computation.19 | custom fusion | flops 3145728 | bytes 7340036 | tf_op jit(solution)/shard_map/scatter-add | solution.py:112
  (73 shorter events, 3.6 us)
Async XLA Ops:
  7.2 21.2 %copy-start = (bf16[2048,512]{1,0:T(8,128)(2,1)S(1)}, bf16[2048,512]{1,0:T(8,128)(2,1)}, u32[]{:S(2)}) copy-start(bf16[2048,512]{1,0:T(8,128)(2,1)} %param.11) | copy-start | bytes 6291460
  7.2 109.6 %all-gather.2.cloned.1.call-start = ((), (), s32[]{:S(2)}) async-start(), calls=%async_computation.3 | async-start | bytes 9437184 | tf_op jit(solution)/shard_map/all_gather | solution.py:73
  41.7 4.8 %copy-start.3 = (bf16[512,512]{1,0:T(8,128)(2,1)S(1)}, bf16[512,512]{1,0:T(8,128)(2,1)}, u32[]{:S(2)}) copy-start(bf16[512,512]{1,0:T(8,128)(2,1)} %param.9) | copy-start | bytes 1572868
  41.7 4.8 %copy-start.4 = (bf16[384,512]{1,0:T(8,128)(2,1)S(1)}, bf16[384,512]{1,0:T(8,128)(2,1)}, u32[]{:S(2)}) copy-start(bf16[384,512]{1,0:T(8,128)(2,1)} %param.8) | copy-start | bytes 1179652
  41.7 58.1 %all-to-all-start.1 = ((bf16[8,384,512]{2,1,0:T(8,128)(2,1)}), bf16[8,384,512]{2,1,0:T(8,128)(2,1)}, u32[]{:S(2)}, u32[]{:S(2)}) async-start(bf16[8,384,512]{2,1,0:T(8,128)(2,1)} %bitcast.83), calls=%async_computation.1 | async-start | bytes 6291456 | tf_op jit(solution)/shard_map/all_to_all | solution.py:50
  47.1 0.9 copy-start.1
  111.1 2.9 copy-start.6
  161.9 148.9 %all-to-all-start.2 = ((bf16[8,384,512]{2,1,0:T(8,128)(2,1)}), bf16[8,384,512]{2,1,0:T(8,128)(2,1)}, u32[]{:S(2)}, u32[]{:S(2)}) async-start(bf16[8,384,512]{2,1,0:T(8,128)(2,1)} %bitcast.82), calls=%async_computation.2 | async-start | bytes 6291456 | tf_op jit(solution)/shard_map/all_to_all | solution.py:106
  166.3 3.8 %copy-start.5 = (bf16[384,512]{1,0:T(8,128)(2,1)S(1)}, bf16[384,512]{1,0:T(8,128)(2,1)}, u32[]{:S(2)}) copy-start(bf16[384,512]{1,0:T(8,128)(2,1)} %param.8) | copy-start | bytes 1179652
  166.3 141.9 %all-reduce.2.cloned.1.call-start = ((), (), s32[]{:S(2)}) async-start(), calls=%async_computation.4 | async-start | bytes 2097152 | tf_op jit(solution)/shard_map/psum | solution.py:114
  166.6 3.5 %copy-start.2 = (f32[384,512]{1,0:T(8,128)S(1)}, f32[384,512]{1,0:T(8,128)}, u32[]{:S(2)}) copy-start(f32[384,512]{1,0:T(8,128)} %copy-done.1) | copy-start | bytes 2359300
Sparse Core Ops, SparseCore 0:
  9.9 81.2 all-gather.1
  172.9 135.2 all-reduce.1
where the time goes:
time: 343 us; the launch traced here: 342 us
  waiting for transfers between devices  113 us (33%)
  blocking collectives  77 us (22%)
  local copies, waits for them, and re-layouts  45.5 us (13%)
  other arithmetic  41.5 us (12%)
  matrix products  38.6 us (11%)
  between operations  16.1 us (5%)
  starting transfers between devices  9.51 us (3%)
    psum x1, waiting for transfers between devices, per_device(): grad_w, loss_sum = lax.psum((grad_local, loss_terms), ('dp', 'lib'))  68.1 us
    psum x1, blocking collectives, per_device(): grad_w, loss_sum = lax.psum((grad_local, loss_terms), ('dp', 'lib'))  67 us
    all_to_all x1, waiting for transfers between devices, per_device(): lax.all_to_all(fetched, 'lib', split_axis=0, concat_axis=0, tiled=True)  44.7 us
    scatter-add x1, other arithmetic, per_device(): grad_mol = jnp.zeros((mol_count, width), jnp.float32).at[received.reshape...  23.2 us
    dot_general x8, matrix products, absorb(): lax.dot_general(spectrum_encoding, block, (((1,), (1,)), ((), ())), prefe...  15.7 us
    dot_general x8, matrix products, absorb(): jnp.dot(weights.astype(jnp.bfloat16), block, preferred_element_type=jnp.f...  15.5 us
    gather x1, local copies, waits for them, and re-layouts, per_device(): fetched = mol_rows[received]  13.3 us
    scatter x1, other arithmetic, per_device(): outgoing = jnp.zeros((lib_size * capacity, width), jnp.bfloat16).at[posit...  10.7 us
  transfers between devices with their start and end apart: 4, of which 2 were waited for; matrix products, arithmetic and copies ran while one was open for 17% of the time, Pallas kernels for 0%

commit v1 on v0

--- a/solution.py
+++ b/solution.py
@@ -111,7 +111,7 @@
         .at[received.reshape(-1)]
         .add(incoming.reshape(-1, width).astype(jnp.float32))
     )
-    grad_w, loss_sum = lax.psum((grad_local, loss_terms), ("dp", "lib"))
+    grad_w, loss_sum = lax.psum(lax.psum((grad_local, loss_terms), axis_name="lib"), "dp")
     loss = loss_sum / (q_rows * lax.axis_size("dp") * lib_size)
     return (grad_w, grad_mol, loss)
 

time: 343 us -> 329 us (0.959)
  blocking collectives: 77 us -> 35.6 us
  waiting for transfers between devices: 113 us -> 141 us
    psum x1 -> x2, blocking collectives: 67 us -> 25.6 us  [the longest x1 13.2 us: per_device(): lax.psum(lax.psum((grad_local, loss_terms), axis_name='lib'), 'dp')]
    psum x1 -> x2, waiting for transfers between devices: 68.1 us -> 95.8 us  [the longest x1 68.9 us: per_device(): lax.psum((grad_local, loss_terms), axis_name='lib')]
  transfers between devices with their start and end apart: 4 -> 5, of which waited for: 2 -> 3; matrix products, arithmetic and copies ran while one was open for 17% -> 17% of each run, Pallas kernels for 0% -> 0%
where the time goes in v1:
time: 329 us; the launch traced here: 328 us
  waiting for transfers between devices  141 us (43%)
  local copies, waits for them, and re-layouts  45.5 us (14%)
  other arithmetic  41.5 us (13%)
  matrix products  38.6 us (12%)
  blocking collectives  35.6 us (11%)
  between operations  15.8 us (5%)
  starting transfers between devices  9.55 us (3%)
    psum x1, waiting for transfers between devices, per_device(): lax.psum((grad_local, loss_terms), axis_name='lib')  68.9 us
    all_to_all x1, waiting for transfers between devices, per_device(): lax.all_to_all(fetched, 'lib', split_axis=0, concat_axis=0, tiled=True)  44.7 us
    psum x1, waiting for transfers between devices, per_device(): lax.psum(lax.psum((grad_local, loss_terms), axis_name='lib'), 'dp')  26.9 us
    scatter-add x1, other arithmetic, per_device(): grad_mol = jnp.zeros((mol_count, width), jnp.float32).at[received.reshape...  23.2 us
    dot_general x8, matrix products, absorb(): lax.dot_general(spectrum_encoding, block, (((1,), (1,)), ((), ())), prefe...  15.7 us
    dot_general x8, matrix products, absorb(): jnp.dot(weights.astype(jnp.bfloat16), block, preferred_element_type=jnp.f...  15.5 us
    gather x1, local copies, waits for them, and re-layouts, per_device(): fetched = mol_rows[received]  13.3 us
    psum x1, blocking collectives, per_device(): lax.psum(lax.psum((grad_local, loss_terms), axis_name='lib'), 'dp')  13.2 us
  transfers between devices with their start and end apart: 5, of which 3 were waited for; matrix products, arithmetic and copies ran while one was open for 17% of the time, Pallas kernels for 0%

profile of v1, /device:TPU:0, one launch (start us, length us, event | category | flops | bytes accessed | tf_op | source)
XLA Modules:
  0.0 328.0 jit_solution(2424028849979133578)
XLA Ops:
  7.2 0.7 all-gather.2.cloned.1.call-update
  7.9 0.8 copy.10
  9.2 2.3 reduce-window.6
  12.2 6.2 %scatter_custom_fusion = s32[3072]{0:T(1024)S(1)} fusion(s32[1536]{0:T(1024)S(1)} %fusion.31, s32[1536]{0:T(1024)S(1)} %get-tuple-element.64, s32[]{:T(128)} %copy.50), kind=kCustom, calls=%fused_computation.91 | custom fusion | bytes 12292 | tf_op jit(solution)/shard_map/scatter | solution.py:46
  18.4 10.0 %all_to_all.22 = s32[8,1,384]{2,1,0:T(1,128)S(1)} all-to-all(s32[8,1,384]{2,1,0:T(1,128)S(1)} %bitcast.85), channel_id=1, replica_groups=mesh['dp'=4,'lib'=8] {'lib'}, dimensions={0} | all-to-all | bytes 24576 | tf_op jit(solution)/shard_map/all_to_all | solution.py:48
  28.4 13.3 %gather_fusion = bf16[3072,512]{1,0:T(8,128)(2,1)} fusion(bf16[2048,512]{1,0:T(8,128)(2,1)S(1)} %copy-done, s32[3072]{0:T(1024)S(1)} %broadcast_clamp_fusion), kind=kCustom, calls=%fused_computation | custom fusion | bytes 6303744 | tf_op jit(solution)/shard_map/gather | solution.py:49
  41.7 4.8 %all-to-all-start.1 = ((bf16[8,384,512]{2,1,0:T(8,128)(2,1)}), bf16[8,384,512]{2,1,0:T(8,128)(2,1)}, u32[]{:S(2)}, u32[]{:S(2)}) async-start(bf16[8,384,512]{2,1,0:T(8,128)(2,1)} %bitcast.83), calls=%async_computation.1 | async-start | bytes 6291456 | tf_op jit(solution)/shard_map/all_to_all | solution.py:50
  46.5 0.5 multiply_reduce_fusion.1
  47.1 0.9 copy-done.1
  48.0 2.2 mul.68
  50.2 4.9 %mul.69 = f32[1536,512]{1,0:T(8,128)} reshape(f32[384,4,512]{2,1,0:T(4,128)} %mul.68) | data formatting | bytes 6291456 | tf_op jit(solution)/shard_map/mul | solution.py:99
  55.1 44.7 %all-to-all-done.1 = bf16[8,384,512]{2,1,0:T(8,128)(2,1)} async-done(((bf16[8,384,512]{2,1,0:T(8,128)(2,1)}), bf16[8,384,512]{2,1,0:T(8,128)(2,1)}, u32[]{:S(2)}, u32[]{:S(2)}) %all-to-all-start.1) | async-done | bytes 3145760 | tf_op jit(solution)/shard_map/all_to_all | solution.py:50
  99.8 7.8 %gather_fusion.1 = bf16[1536,512]{1,0:T(8,128)(2,1)} fusion(bf16[3072,512]{1,0:T(8,128)(2,1)} %bitcast.7, s32[2048]{0:T(1024)S(1)} %pad_clamp_fusion), kind=kCustom, calls=%fused_computation.1 | custom fusion | bytes 3151872 | tf_op jit(solution)/shard_map/gather | solution.py:51
  107.6 3.5 %reshape.274 = bf16[384,4,512]{2,1,0:T(4,128)(2,1)} reshape(bf16[1536,512]{1,0:T(8,128)(2,1)} %gather_fusion.1) | data formatting | bytes 3145728 | tf_op jit(solution)/shard_map/reshape | solution.py:51
  111.1 2.8 fusion.18
  114.3 2.4 fusion.43
  116.8 34.0 %while.14 = (s32[]{:T(128)}, f32[384]{0:T(512)S(1)}, f32[384]{0:T(512)S(1)}, f32[384,512]{1,0:T(8,128)S(1)}, bf16[8,1024,512]{2,1,0:T(8,128)(2,1)}, /*index=5*/bf16[384,512]{1,0:T(8,128)(2,1)S(1)}, s32[]{:T(128)}) while((s32[]{:T(128)}, f32[384]{0:T(512)S(1)}, f32[384]{0:T(512)S(1)}, f32[384,512]{1,0:T(8,128)S(1)}, ...), condition=%wide.region_10.11_spmd, body=%wide.region_7.10_spmd.sunk | while | flops 808059648 | bytes 8806493 | solution.py:79
  116.8 2.0 fusion.59
  118.8 0.3 fusion.60
  119.1 1.9 convolution_add_fusion.2
  121.1 2.0 fusion.59
  123.3 1.9 convolution_add_fusion.2
  125.3 2.0 fusion.59
  127.6 1.9 convolution_add_fusion.2
  129.6 2.0 fusion.59
  131.8 1.9 convolution_add_fusion.2
  133.8 2.0 fusion.59
  136.1 1.9 convolution_add_fusion.2
  138.1 2.0 fusion.59
  140.0 0.3 fusion.60
  140.4 1.9 convolution_add_fusion.2
  142.3 2.0 fusion.59
  144.6 1.9 convolution_add_fusion.2
  146.6 2.0 fusion.59
  148.5 0.3 fusion.60
  148.9 1.9 convolution_add_fusion.2
  151.2 10.7 %scatter_custom_fusion.1 = bf16[3072,512]{1,0:T(8,128)(2,1)} fusion(s32[1536]{0:T(1024)S(1)} %fusion.31, f32[1536,512]{1,0:T(8,128)} %mul.69, f32[]{:T(128)} %constant.84.clone.1, f32[1536]{0:T(1024)S(1)} %mul.66, bf16[]{:T(256)} %constant.87.clone.1), kind=kCustom, calls=%fused_computation.23 | custom fusion | flops 2359296 | bytes 6299654 | tf_op jit(solution)/shard_map/scatter | solution.py:104
  161.9 4.4 %all-to-all-start.2 = ((bf16[8,384,512]{2,1,0:T(8,128)(2,1)}), bf16[8,384,512]{2,1,0:T(8,128)(2,1)}, u32[]{:S(2)}, u32[]{:S(2)}) async-start(bf16[8,384,512]{2,1,0:T(8,128)(2,1)} %bitcast.82), calls=%async_computation.2 | async-start | bytes 6291456 | tf_op jit(solution)/shard_map/all_to_all | solution.py:106
  166.4 2.0 slice.22
  168.4 1.4 multiply_reduce_fusion
  169.9 1.7 convolution_bitcast_fusion
  171.9 68.9 %all-reduce.3.cloned.1.call-done = f32[512,512]{0,1:T(8,128)} async-done(((f32[512,512]{0,1:T(8,128)}), f32[512,512]{0,1:T(8,128)}) %all-reduce.3.cloned.1.call-update) | async-done | bytes 1048592 | tf_op jit(solution)/shard_map/psum | solution.py:114
  240.8 0.6 subtract_reduce_fusion
  241.4 12.5 %psum.30 = f32[]{:T(128)} all-reduce(f32[]{:T(128)} %subtract_reduce_fusion), channel_id=1, replica_groups=mesh['dp'=4,'lib'=8] {'lib'}, use_global_device_ids=true, to_apply=%region_17.18 | all-reduce | flops 1 | bytes 8 | tf_op jit(solution)/shard_map/psum | solution.py:114
  253.9 13.2 %psum.31 = f32[]{:T(128)} all-reduce(f32[]{:T(128)} %psum.30), channel_id=1, replica_groups=mesh['dp'=4,'lib'=8] {'dp'}, use_global_device_ids=true, to_apply=%region_18.19 | all-reduce | flops 1 | bytes 8 | tf_op jit(solution)/shard_map/psum | solution.py:114
  267.7 26.9 %all-reduce.5.cloned.1.call-done = f32[512,512]{0,1:T(8,128)} async-done(((f32[512,512]{0,1:T(8,128)}), f32[512,512]{0,1:T(8,128)}) %all-reduce.5.cloned.1.call-update) | async-done | bytes 1048592 | tf_op jit(solution)/shard_map/psum | solution.py:114
  294.6 2.5 copy.15
  297.1 23.2 %scatter_custom_fusion.2 = f32[2048,512]{1,0:T(8,128)} fusion(s32[3072]{0:T(1024)S(1)} %bitcast.88, bf16[3072,512]{1,0:T(8,128)(2,1)} %bitcast.19, f32[]{:T(128)} %constant.73.clone.1), kind=kCustom, calls=%fused_computation.19 | custom fusion | flops 3145728 | bytes 7340036 | tf_op jit(solution)/shard_map/scatter-add | solution.py:112
  (77 shorter events, 4.2 us)
Async XLA Ops:
  7.2 21.2 %copy-start = (bf16[2048,512]{1,0:T(8,128)(2,1)S(1)}, bf16[2048,512]{1,0:T(8,128)(2,1)}, u32[]{:S(2)}) copy-start(bf16[2048,512]{1,0:T(8,128)(2,1)} %param.11) | copy-start | bytes 6291460
  7.2 109.6 %all-gather.2.cloned.1.call-start = ((), (), s32[]{:S(2)}) async-start(), calls=%async_computation.3 | async-start | bytes 9437184 | tf_op jit(solution)/shard_map/all_gather | solution.py:73
  41.7 4.8 %copy-start.3 = (bf16[512,512]{1,0:T(8,128)(2,1)S(1)}, bf16[512,512]{1,0:T(8,128)(2,1)}, u32[]{:S(2)}) copy-start(bf16[512,512]{1,0:T(8,128)(2,1)} %param.9) | copy-start | bytes 1572868
  41.7 4.8 %copy-start.4 = (bf16[384,512]{1,0:T(8,128)(2,1)S(1)}, bf16[384,512]{1,0:T(8,128)(2,1)}, u32[]{:S(2)}) copy-start(bf16[384,512]{1,0:T(8,128)(2,1)} %param.8) | copy-start | bytes 1179652
  41.7 58.1 %all-to-all-start.1 = ((bf16[8,384,512]{2,1,0:T(8,128)(2,1)}), bf16[8,384,512]{2,1,0:T(8,128)(2,1)}, u32[]{:S(2)}, u32[]{:S(2)}) async-start(bf16[8,384,512]{2,1,0:T(8,128)(2,1)} %bitcast.83), calls=%async_computation.1 | async-start | bytes 6291456 | tf_op jit(solution)/shard_map/all_to_all | solution.py:50
  47.1 0.9 copy-start.1
  111.1 2.9 copy-start.6
  161.9 135.2 %all-to-all-start.2 = ((bf16[8,384,512]{2,1,0:T(8,128)(2,1)}), bf16[8,384,512]{2,1,0:T(8,128)(2,1)}, u32[]{:S(2)}, u32[]{:S(2)}) async-start(bf16[8,384,512]{2,1,0:T(8,128)(2,1)} %bitcast.82), calls=%async_computation.2 | async-start | bytes 6291456 | tf_op jit(solution)/shard_map/all_to_all | solution.py:106
  166.3 3.5 %copy-start.5 = (bf16[384,512]{1,0:T(8,128)(2,1)S(1)}, bf16[384,512]{1,0:T(8,128)(2,1)}, u32[]{:S(2)}) copy-start(bf16[384,512]{1,0:T(8,128)(2,1)} %param.8) | copy-start | bytes 1179652
  166.3 74.4 %all-reduce.3.cloned.1.call-start = ((), (), s32[]{:S(2)}) async-start(), calls=%async_computation.4 | async-start | bytes 2097152 | tf_op jit(solution)/shard_map/psum | solution.py:114
  166.4 3.5 %copy-start.2 = (f32[384,512]{1,0:T(8,128)S(1)}, f32[384,512]{1,0:T(8,128)}, u32[]{:S(2)}) copy-start(f32[384,512]{1,0:T(8,128)} %copy-done.1) | copy-start | bytes 2359300
  171.6 123.0 %all-reduce.5.cloned.1.call-start = ((), (), s32[]{:S(2)}) async-start(), calls=%async_computation.5 | async-start | bytes 2097152 | tf_op jit(solution)/shard_map/psum | solution.py:114
Sparse Core Ops, SparseCore 0:
  9.9 81.2 all-gather.1
  171.7 68.9 all-reduce.2
  243.1 51.3 all-reduce.4
